TPU v7x, 32 devices: a whole 2x2x4 slice. The times are simulated.
32 devices in a mesh: fsdp: 4 (over y, x), seq: 8 (over z, core).
Axes of the slice: x: 2, y: 2, z: 4, core: 2. Of those that a mesh axis runs over, the one named last changes fastest.
Arguments:
- residual_in: bfloat16 [4, 1024, 2048], P('fsdp', 'seq'), may hold values from -6 to 6
- attn_gain: bfloat16 [2048], replicated, may hold values from 0.5 to 1.5
- mlp_gain: bfloat16 [2048], replicated, may hold values from 0.5 to 1.5
- w_qkv: bfloat16 [2048, 3, 2048], P('fsdp'), may hold values from -0.125 to 0.125
- w_out: bfloat16 [2048, 2048], P('fsdp'), may hold values from -1 to 1
- w_gate_up: bfloat16 [8192, 2, 2048], P('fsdp'), may hold values from -0.125 to 0.125
- w_down: bfloat16 [2048, 8192], P('fsdp'), may hold values from -0.0625 to 0.0625
- cotangent: bfloat16 [4, 1024, 2048], P('fsdp', 'seq'), may hold values from -6 to 6
Outputs:
- layer_out: bfloat16 [4, 1024, 2048], P('fsdp', 'seq')
- grad_input: float32 [4, 1024, 2048], P('fsdp', 'seq')
- grad_attn_gain: float32 [2048], P(('fsdp', 'seq'))
- grad_mlp_gain: float32 [2048], P(('fsdp', 'seq'))
- grad_qkv: float32 [2048, 3, 2048], P(('seq', 'fsdp'))
- grad_out_proj: float32 [2048, 2048], P(None, ('seq', 'fsdp'))
- grad_gate_up: float32 [8192, 2, 2048], P(('seq', 'fsdp'))
- grad_down: float32 [2048, 8192], P(None, ('seq', 'fsdp'))
All inputs are finite; a program needn't handle non-finite values.
Results may differ from a plain program's by a relative error of at most 0.018.
Values may be sent and summed in bfloat16 or wider, within the bound.
No kernel may reach another device: no remote copies, remote signals or barrier semaphores. Data moves between devices by JAX's collectives and lax.ppermute only.
A program may use at most 384 MiB of HBM per device.

v0:
```python
import math
import jax
import jax.numpy as jnp
from jax import lax
from jax.sharding import PartitionSpec as P

HD = 64
NORM_EPS = 1e-05
ROPE_BASE = 130000.0


def rotate(matrix):
    shaped = matrix.reshape(matrix.shape[:-1] + (matrix.shape[-1] // HD, 2, HD // 2))
    turned = jnp.stack([-shaped[..., 1, :], shaped[..., 0, :]], axis=-2)
    return turned.reshape(matrix.shape)


def rotate_back(matrix):
    shaped = matrix.reshape(matrix.shape[:-1] + (matrix.shape[-1] // HD, 2, HD // 2))
    turned = jnp.stack([shaped[..., 1, :], -shaped[..., 0, :]], axis=-2)
    return turned.reshape(matrix.shape)


def rope_tables(positions, columns):
    freq_index = (jnp.arange(columns, dtype=jnp.int32) % (HD // 2)).astype(jnp.float32)
    inverse = ROPE_BASE ** (-2.0 * freq_index / HD)
    angles = positions.astype(jnp.float32)[:, None] * inverse[None, :]
    return (jnp.cos(angles), jnp.sin(angles))


def rms_scale(matrix):
    return lax.rsqrt(jnp.mean(matrix * matrix, axis=-1, keepdims=True) + NORM_EPS)


def rms_back(grad_normed, matrix, scale_rows, gain):
    weighted = grad_normed * gain
    inner_mean = jnp.mean(weighted * matrix, axis=-1, keepdims=True)
    grad_matrix = scale_rows * weighted - matrix * scale_rows**3 * inner_mean
    grad_gain = jnp.sum(grad_normed * matrix * scale_rows, axis=0)
    return (grad_matrix, grad_gain)


def attend_forward(queries, key_rows, values):
    seq_count, length, width_here = queries.shape
    heads_here = width_here // HD
    q_block = min(512, length)
    k_block = min(256, length)
    inv_root = 1.0 / math.sqrt(HD)
    shaped_q = queries.reshape(seq_count, length, heads_here, HD)
    shaped_k = key_rows.reshape(seq_count, length, heads_here, HD)
    shaped_v = values.reshape(seq_count, length, heads_here, HD)

    def query_step(q_index, carried):
        attended, totals = carried
        offset = q_index * q_block
        q_rows = lax.dynamic_slice_in_dim(shaped_q, offset, q_block, 1)
        query_pos = offset + jnp.arange(q_block, dtype=jnp.int32)

        def key_step(k_index, running):
            unnorm, denominator = running
            k_start = k_index * k_block
            k_rows = lax.dynamic_slice_in_dim(shaped_k, k_start, k_block, 1)
            v_rows = lax.dynamic_slice_in_dim(shaped_v, k_start, k_block, 1)
            scores = (
                jnp.einsum("bqhd,bkhd->bhqk", q_rows, k_rows, preferred_element_type=jnp.float32)
                * inv_root
            )
            causal = (k_start + jnp.arange(k_block, dtype=jnp.int32))[None, :] <= query_pos[:, None]
            exp_scores = jnp.where(causal, jnp.exp(scores), 0.0)
            denominator = denominator + jnp.sum(exp_scores, axis=-1)
            unnorm = unnorm + jnp.einsum(
                "bhqk,bkhd->bqhd",
                exp_scores.astype(jnp.bfloat16),
                v_rows,
                preferred_element_type=jnp.float32,
            )
            return (unnorm, denominator)

        start_state = (
            jnp.zeros((seq_count, q_block, heads_here, HD), jnp.float32),
            jnp.zeros((seq_count, heads_here, q_block), jnp.float32),
        )
        unnorm, denominator = lax.fori_loop(0, (offset + q_block) // k_block, key_step, start_state)
        block_out = unnorm / jnp.transpose(denominator, (0, 2, 1))[..., None]
        attended = lax.dynamic_update_slice_in_dim(attended, block_out, offset, 1)
        totals = lax.dynamic_update_slice_in_dim(totals, denominator, offset, 2)
        return (attended, totals)

    initial = (
        jnp.zeros((seq_count, length, heads_here, HD), jnp.float32),
        jnp.zeros((seq_count, heads_here, length), jnp.float32),
    )
    attended, totals = lax.fori_loop(0, length // q_block, query_step, initial)
    return (attended.reshape(seq_count, length, width_here), totals)


def attend_backward(queries, key_rows, values, attended, totals, grad_attended):
    seq_count, length, width_here = queries.shape
    heads_here = width_here // HD
    q_block = min(512, length)
    k_block = min(256, length)
    inv_root = 1.0 / math.sqrt(HD)
    shaped_q = queries.reshape(seq_count, length, heads_here, HD)
    shaped_k = key_rows.reshape(seq_count, length, heads_here, HD)
    shaped_v = values.reshape(seq_count, length, heads_here, HD)
    shaped_grad = grad_attended.reshape(seq_count, length, heads_here, HD).astype(jnp.float32)
    shaped_att = attended.reshape(seq_count, length, heads_here, HD)
    totals_rows = jnp.transpose(totals, (0, 2, 1))
    grad_total = -jnp.sum(shaped_grad * shaped_att, axis=-1) / totals_rows
    grad_unnorm = (shaped_grad / totals_rows[..., None]).astype(jnp.bfloat16)

    def query_step(q_index, carried):
        grad_q, grad_k, grad_v = carried
        offset = q_index * q_block
        q_rows = lax.dynamic_slice_in_dim(shaped_q, offset, q_block, 1)
        g_rows = lax.dynamic_slice_in_dim(grad_unnorm, offset, q_block, 1)
        total_rows = jnp.transpose(
            lax.dynamic_slice_in_dim(grad_total, offset, q_block, 1), (0, 2, 1)
        )
        query_pos = offset + jnp.arange(q_block, dtype=jnp.int32)

        def key_step(k_index, running):
            dq_acc, dk_all, dv_all = running
            k_start = k_index * k_block
            k_rows = lax.dynamic_slice_in_dim(shaped_k, k_start, k_block, 1)
            v_rows = lax.dynamic_slice_in_dim(shaped_v, k_start, k_block, 1)
            scores = (
                jnp.einsum("bqhd,bkhd->bhqk", q_rows, k_rows, preferred_element_type=jnp.float32)
                * inv_root
            )
            causal = (k_start + jnp.arange(k_block, dtype=jnp.int32))[None, :] <= query_pos[:, None]
            exp_scores = jnp.where(causal, jnp.exp(scores), 0.0)
            grad_prob = jnp.einsum(
                "bqhd,bkhd->bhqk", g_rows, v_rows, preferred_element_type=jnp.float32
            )
            grad_scores = (exp_scores * (grad_prob + total_rows[..., None])).astype(jnp.bfloat16)
            dq_acc = (
                dq_acc
                + jnp.einsum(
                    "bhqk,bkhd->bqhd", grad_scores, k_rows, preferred_element_type=jnp.float32
                )
                * inv_root
            )
            dk_part = (
                jnp.einsum(
                    "bhqk,bqhd->bkhd", grad_scores, q_rows, preferred_element_type=jnp.float32
                )
                * inv_root
            )
            dv_part = jnp.einsum(
                "bhqk,bqhd->bkhd",
                exp_scores.astype(jnp.bfloat16),
                g_rows,
                preferred_element_type=jnp.float32,
            )
            dk_slice = lax.dynamic_slice_in_dim(dk_all, k_start, k_block, 1) + dk_part
            dv_slice = lax.dynamic_slice_in_dim(dv_all, k_start, k_block, 1) + dv_part
            dk_all = lax.dynamic_update_slice_in_dim(dk_all, dk_slice, k_start, 1)
            dv_all = lax.dynamic_update_slice_in_dim(dv_all, dv_slice, k_start, 1)
            return (dq_acc, dk_all, dv_all)

        start_state = (jnp.zeros((seq_count, q_block, heads_here, HD), jnp.float32), grad_k, grad_v)
        dq_block, grad_k, grad_v = lax.fori_loop(
            0, (offset + q_block) // k_block, key_step, start_state
        )
        grad_q = lax.dynamic_update_slice_in_dim(grad_q, dq_block, offset, 1)
        return (grad_q, grad_k, grad_v)

    empty = jnp.zeros((seq_count, length, heads_here, HD), jnp.float32)
    grad_q, grad_k, grad_v = lax.fori_loop(0, length // q_block, query_step, (empty, empty, empty))
    cosine, sine_table = rope_tables(jnp.arange(length, dtype=jnp.int32), width_here)
    grad_q = grad_q.reshape(seq_count, length, width_here)
    grad_k = grad_k.reshape(seq_count, length, width_here)
    grad_v = grad_v.reshape(seq_count, length, width_here)
    raw_q = grad_q * cosine + rotate_back(grad_q * sine_table)
    raw_k = grad_k * cosine + rotate_back(grad_k * sine_table)
    return jnp.stack([raw_q, raw_k, grad_v]).astype(jnp.bfloat16)


def body(residual_in, attn_gain, mlp_gain, w_qkv, w_out, w_gate_up, w_down, cotangent):
    seq_count, shard_len, model_width = residual_in.shape
    tokens = seq_count * shard_len
    seq_index = lax.axis_index("seq")
    positions = seq_index * shard_len + jnp.arange(tokens, dtype=jnp.int32) % shard_len
    cosine, sine_table = rope_tables(positions, model_width)
    inputs = residual_in.reshape(tokens, model_width).astype(jnp.float32)
    gain_one = attn_gain.astype(jnp.float32)
    gain_two = mlp_gain.astype(jnp.float32)
    scale_one = rms_scale(inputs)
    normed_one = (inputs * scale_one * gain_one).astype(jnp.bfloat16)
    qkv_full, out_full = (
        lax.all_gather(w_qkv, "fsdp", axis=0, tiled=True),
        lax.all_gather(w_out, "fsdp", axis=0, tiled=True),
    )
    projected = jnp.einsum("td,fpd->ptf", normed_one, qkv_full, preferred_element_type=jnp.float32)
    queries = (projected[0] * cosine + rotate(projected[0]) * sine_table).astype(jnp.bfloat16)
    key_rows = (projected[1] * cosine + rotate(projected[1]) * sine_table).astype(jnp.bfloat16)
    values = projected[2].astype(jnp.bfloat16)
    stacked = jnp.stack([queries, key_rows, values]).reshape(3, seq_count, shard_len, model_width)
    head_view = lax.all_to_all(stacked, "seq", split_axis=3, concat_axis=2, tiled=True)
    attended, totals = attend_forward(head_view[0], head_view[1], head_view[2])
    attended_heads = attended.astype(jnp.bfloat16)
    sent_back = lax.all_to_all(attended_heads, "seq", split_axis=1, concat_axis=2, tiled=True)
    attended_low = sent_back.reshape(tokens, model_width)
    branch = jnp.einsum("ti,fi->tf", attended_low, out_full, preferred_element_type=jnp.float32)
    residual = inputs + branch
    scale_two = rms_scale(residual)
    normed_two = (residual * scale_two * gain_two).astype(jnp.bfloat16)
    up_full, down_full = (
        lax.all_gather(w_gate_up, "fsdp", axis=0, tiled=True),
        lax.all_gather(w_down, "fsdp", axis=0, tiled=True),
    )
    gate_up = jnp.einsum("td,jpd->ptj", normed_two, up_full, preferred_element_type=jnp.float32)
    hidden = (jax.nn.silu(gate_up[0]) * gate_up[1]).astype(jnp.bfloat16)
    mlp_term = jnp.einsum("tj,fj->tf", hidden, down_full, preferred_element_type=jnp.float32)
    layer_out = (
        (residual + mlp_term).astype(jnp.bfloat16).reshape(seq_count, shard_len, model_width)
    )
    grad_out = cotangent.reshape(tokens, model_width)
    up_again, down_again = (
        lax.all_gather(w_gate_up, "fsdp", axis=0, tiled=True),
        lax.all_gather(w_down, "fsdp", axis=0, tiled=True),
    )
    grad_hidden = jnp.einsum("tf,fj->tj", grad_out, down_again, preferred_element_type=jnp.float32)
    sigmoid_gate = jax.nn.sigmoid(gate_up[0])
    grad_gate = grad_hidden * gate_up[1] * sigmoid_gate * (1.0 + gate_up[0] * (1.0 - sigmoid_gate))
    grad_up = grad_hidden * jax.nn.silu(gate_up[0])
    grad_gu = jnp.stack([grad_gate, grad_up]).astype(jnp.bfloat16)
    grad_normed_two = jnp.einsum(
        "ptj,jpd->td", grad_gu, up_again, preferred_element_type=jnp.float32
    )
    ff_width = grad_gu.shape[2]
    unit_rows = jnp.concatenate([grad_gu, hidden[None]], axis=0).reshape(
        3, seq_count, shard_len, ff_width
    )
    unit_cols = lax.all_to_all(unit_rows, "seq", split_axis=3, concat_axis=2, tiled=True)
    normed_piece = lax.all_gather(
        normed_two.reshape(seq_count, shard_len, model_width), "seq", axis=1, tiled=True
    )
    grad_piece = lax.all_gather(cotangent, "seq", axis=1, tiled=True)
    gu_part = jnp.einsum(
        "psnj,snd->jpd", unit_cols[:2], normed_piece, preferred_element_type=jnp.float32
    )
    down_part = jnp.einsum(
        "snf,snj->fj", grad_piece, unit_cols[2], preferred_element_type=jnp.float32
    )
    gu_part, down_part = (gu_part, down_part)
    grad_gate_up, grad_down = (
        lax.psum_scatter(
            gu_part.astype(jnp.bfloat16), "fsdp", scatter_dimension=0, tiled=True
        ).astype(jnp.float32),
        lax.psum_scatter(
            down_part.astype(jnp.bfloat16), "fsdp", scatter_dimension=1, tiled=True
        ).astype(jnp.float32),
    )
    grad_norm_two, grad_gain_two = rms_back(grad_normed_two, residual, scale_two, gain_two)
    grad_residual = grad_out.astype(jnp.float32) + grad_norm_two
    qkv_back, out_back = (
        lax.all_gather(w_qkv, "fsdp", axis=0, tiled=True),
        lax.all_gather(w_out, "fsdp", axis=0, tiled=True),
    )
    grad_branch = grad_residual.astype(jnp.bfloat16)
    grad_attended = jnp.einsum(
        "tf,fi->ti", grad_branch, out_back, preferred_element_type=jnp.float32
    )
    grad_attended = grad_attended.astype(jnp.bfloat16).reshape(seq_count, shard_len, model_width)
    grad_heads = lax.all_to_all(grad_attended, "seq", split_axis=2, concat_axis=1, tiled=True)
    grad_stacked = attend_backward(
        head_view[0], head_view[1], head_view[2], attended, totals, grad_heads
    )
    normed_piece = lax.all_gather(
        normed_one.reshape(seq_count, shard_len, model_width), "seq", axis=1, tiled=True
    )
    branch_piece = lax.all_gather(
        grad_branch.reshape(seq_count, shard_len, model_width), "seq", axis=1, tiled=True
    )
    grad_piece = grad_stacked
    qkv_part = jnp.einsum(
        "psnf,snd->fpd", grad_piece, normed_piece, preferred_element_type=jnp.float32
    )
    out_part = jnp.einsum(
        "snf,sni->fi", branch_piece, attended_heads, preferred_element_type=jnp.float32
    )
    qkv_part, out_part = (qkv_part, out_part)
    grad_qkv, grad_out_proj = (
        lax.psum_scatter(
            qkv_part.astype(jnp.bfloat16), "fsdp", scatter_dimension=0, tiled=True
        ).astype(jnp.float32),
        lax.psum_scatter(
            out_part.astype(jnp.bfloat16), "fsdp", scatter_dimension=1, tiled=True
        ).astype(jnp.float32),
    )
    grad_projected = lax.all_to_all(grad_stacked, "seq", split_axis=2, concat_axis=3, tiled=True)
    grad_projected = grad_projected.reshape(3, tokens, model_width)
    grad_normed_one = jnp.einsum(
        "ptf,fpd->td", grad_projected, qkv_back, preferred_element_type=jnp.float32
    )
    grad_norm_one, grad_gain_one = rms_back(grad_normed_one, inputs, scale_one, gain_one)
    grad_input = (grad_residual + grad_norm_one).reshape(seq_count, shard_len, model_width)
    grad_attn_gain, grad_mlp_gain = (
        lax.psum_scatter(grad_gain_one, ("fsdp", "seq"), scatter_dimension=0, tiled=True),
        lax.psum_scatter(grad_gain_two, ("fsdp", "seq"), scatter_dimension=0, tiled=True),
    )
    return (
        layer_out,
        grad_input,
        grad_attn_gain,
        grad_mlp_gain,
        grad_qkv,
        grad_out_proj,
        grad_gate_up,
        grad_down,
    )


def solution(mesh):
    return jax.shard_map(
        body,
        mesh=mesh,
        in_specs=(
            P("fsdp", "seq", None),
            P(),
            P(),
            P("fsdp", None, None),
            P("fsdp", None),
            P("fsdp", None, None),
            P("fsdp", None),
            P("fsdp", "seq", None),
        ),
        out_specs=(
            P("fsdp", "seq", None),
            P("fsdp", "seq", None),
            P(("fsdp", "seq")),
            P(("fsdp", "seq")),
            P(("seq", "fsdp"), None, None),
            P(None, ("seq", "fsdp")),
            P(("seq", "fsdp"), None, None),
            P(None, ("seq", "fsdp")),
        ),
        check_vma=False,
    )
```

profile of v0, /device:TPU:0, one launch (start us, length us, event | category | flops | bytes accessed | tf_op | source)
XLA Modules:
  0.0 1827.8 jit_solution(5378411040820716253)
XLA Ops:
  8.7 18.1 copy.202
  28.7 211.5 %all-gather.11.cloned.1.call-done = bf16[2048,3,2048]{2,0,1:T(8,128)(2,1)} async-done(((bf16[512,3,2048]{2,0,1:T(8,128)(2,1)}), bf16[2048,3,2048]{2,0,1:T(8,128)(2,1)}) %all-gather.11.cloned.1.call-update) | async-done | bytes 25165840 | tf_op jit(solution)/shard_map/all_gather | solution.py:192
  240.2 13.5 convolution_bitcast_fusion.3
  256.0 2.5 copy.192
  260.9 2.5 copy.193
  263.4 2.5 copy.194
  268.3 2.5 copy.195
  270.8 5.3 fusion.111
  276.4 2.5 copy.196
  278.9 5.1 all-to-all-start
  284.0 49.0 %all-to-all-done = bf16[3,1,128,2048]{2,0,1,3:T(4,128)(2,1)S(1)} async-done(((bf16[3,1,128,2048]{2,0,1,3:T(4,128)(2,1)}), bf16[3,1,128,2048]{2,0,1,3:T(4,128)(2,1)S(1)}, u32[]{:S(2)}, u32[]{:S(2)}) %all-to-all-start) | async-done | bytes 1572896 | tf_op jit(solution)/shard_map/all_to_all | solution.py:200
  333.0 3.2 fusion.142
  340.4 17.2 while.118
  341.2 5.1 while.121
  347.3 10.2 while.121
  358.5 3.6 copy.200
  362.7 5.9 reduce.3
  370.7 4.1 all-to-all-start.1
  376.2 14.0 all-to-all-done.1
  395.3 6.5 multiply_reduce_fusion.3
  402.0 506.1 %all-gather.15.cloned.1.call-done = bf16[8192,2,2048]{2,0,1:T(8,128)(2,1)} async-done(((bf16[2048,2,2048]{2,0,1:T(8,128)(2,1)}), bf16[8192,2,2048]{2,0,1:T(8,128)(2,1)}) %all-gather.15.cloned.1.call-update) | async-done | bytes 67108880 | tf_op jit(solution)/shard_map/all_gather | solution.py:210
  908.1 37.6 %convolution_bitcast_fusion.2 = f32[2,128,8192]{2,1,0:T(8,128)} fusion(bf16[8192,2,2048]{2,0,1:T(8,128)(2,1)} %all-gather.15.cloned.1.call-done, bf16[128,2048]{1,0:T(8,128)(2,1)S(1)} %multiply_convert_fusion.2), kind=kOutput, calls=%fused_computation.67 | convolution fusion | flops 8589934592 | bytes 76021760 | tf_op jit(solution)/shard_map/td,jpd->ptj/dot_general | solution.py:213
  945.7 261.2 %all-gather.17.cloned.1.call-done = bf16[2048,8192]{1,0:T(8,128)(2,1)} async-done(((bf16[512,8192]{1,0:T(8,128)(2,1)}), bf16[2048,8192]{1,0:T(8,128)(2,1)}) %all-gather.17.cloned.1.call-update) | async-done | bytes 33554448 | tf_op jit(solution)/shard_map/all_gather | solution.py:211
  1206.9 19.1 %fusion.83 = (bf16[1,128,8192]{2,1,0:T(8,128)(2,1)}, bf16[1,128,8192]{2,1,0:T(8,128)(2,1)}) fusion(f32[2,128,8192]{2,1,0:T(8,128)} %convolution_bitcast_fusion.2, bf16[2048,8192]{1,0:T(8,128)(2,1)} %all-gather.17.cloned.1.call-done, bf16[1,128,2048]{2,1,0:T(8,128)(2,1)} %param.23), kind=kOutput, calls=%fused_computation.108 | convolution fusion | flops 4308598784 | bytes 46661632 | tf_op jit(solution)/shard_map/tf,fj->tj/dot_general | solution.py:224
  1226.0 25.3 %multiply_reduce_fusion = (f32[2048]{0:T(1024)}, f32[128]{0:T(128)S(1)}, f32[128,2048]{1,0:T(8,128)S(1)}) fusion(f32[128,2048]{1,0:T(8,128)S(1)} %get-tuple-element.716, f32[128]{0:T(128)S(1)} %get-tuple-element.714, f32[2048]{0:T(1024)S(1)} %convert_element_type.212, bf16[8192,2,2048]{2,0,1:T(8,128)(2,1)} %all-gather.15.cloned.1.call-done, ...), kind=kOutput, calls=%fused_computation.151 | convolution fusion | flops 8593602560 | bytes 73417728 | tf_op jit(solution)/shard_map/ptj,jpd->td/dot_general | solution.py:229
  1254.4 6.0 multiply_convert_fusion
  1260.3 4.9 fusion.79
  1266.0 11.5 reduce.4
  1278.4 4.5 all-to-all-start.2
  1282.9 6.5 maximum_bitcast_fusion
  1289.4 13.2 copy.216
  1302.6 8.8 all-to-all-done.2
  1311.3 4.9 all-to-all-start.4
  1322.3 2.6 reshape.859
  1324.8 2.3 multiply_reduce_fusion.1
  1329.4 37.3 %while.120 = (s32[]{:T(128)}, f32[1,1024,4,64]{1,3,2,0:T(8,128)}, f32[1,1024,4,64]{1,3,2,0:T(8,128)S(1)}, f32[1,1024,4,64]{1,3,2,0:T(8,128)}, bf16[1,1024,4,64]{...) while((s32[]{:T(128)}, f32[1,1024,4,64]{1,3,2,0:T(8,128)}, ...), condition=%wide.region_12.13_spmd, body=%wide.region_9.12_spmd.sunk | while | flops 340329248 | bytes 17070880 | solution.py:170
  1331.2 10.7 while.122
  1344.5 21.4 %while.122 = (s32[]{:T(128)}, f32[1,512,4,64]{1,3,2,0:T(8,128)S(1)}, f32[1,1024,4,64]{1,3,2,0:T(8,128)S(1)}, f32[1,1024,4,64]{1,3,2,0:T(8,128)}, s32[]{:T(128)},...) while((s32[]{:T(128)}, f32[1,512,4,64]{1,3,2,0:T(8,128)S(1)}, ...), condition=%wide.region_11.11_spmd.clone, body=%wide.region_10.10_spmd.clone.sunk | while | flops 340329216 | bytes 14432507 | solution.py:163
  1368.0 4.7 fusion.115
  1374.8 2.5 copy.206
  1380.8 2.6 copy.208
  1384.9 5.2 add_convert_fusion.1
  1390.2 7.5 fusion.72
  1397.7 7.8 copy.215
  1405.6 4.4 convolution_convert_fusion
  1410.0 157.5 %all-to-all-done.4 = bf16[3,1,128,8192]{2,0,1,3:T(4,128)(2,1)} async-done(((bf16[3,1,128,8192]{2,0,1,3:T(4,128)(2,1)}), bf16[3,1,128,8192]{2,0,1,3:T(4,128)(2,1)}, u32[]{:S(2)}, u32[]{:S(2)}) %all-to-all-start.4) | async-done | bytes 6291488 | tf_op jit(solution)/shard_map/all_to_all | solution.py:236
  1567.5 4.6 copy.217
  1572.1 2.7 copy-done
  1574.9 2.6 copy.220
  1577.6 9.5 convert_bitcast_fusion.1
  1587.1 4.6 slice.103
  1591.7 6.3 copy.218
  1598.0 14.1 convert_bitcast_fusion
  1613.5 2.7 copy.210
  1616.2 3.8 all-to-all-start.3
  1621.3 19.0 %fusion.80 = bf16[1,128,2048]{2,1,0:T(8,128)(2,1)} fusion(f32[128,2048]{1,0:T(8,128)S(1)} %copy-done.5, bf16[2048,8192]{1,0:T(8,128)(2,1)} %all-gather.17.cloned.1.call-done, f32[2,128,8192]{2,1,0:T(8,128)} %convolution_bitcast_fusion.2), kind=kOutput, calls=%fused_computation.106 | convolution fusion | flops 4301783040 | bytes 43515904 | tf_op jit(solution)/shard_map/tj,fj->tf/dot_general | solution.py:215
  1640.2 28.7 %all-to-all-done.3 = bf16[3,1,1024,256]{3,0,1,2:T(4,128)(2,1)S(1)} async-done(((bf16[3,1,1024,256]{3,0,1,2:T(4,128)(2,1)}), bf16[3,1,1024,256]{3,0,1,2:T(4,128)(2,1)S(1)}, u32[]{:S(2)}, u32[]{:S(2)}) %all-to-all-start.3) | async-done | bytes 1572896 | tf_op jit(solution)/shard_map/all_to_all | solution.py:293
  1671.2 2.6 reshape.847
  1673.8 13.6 fusion.107
  1687.4 38.0 %all-reduce.3 = (f32[2048]{0:T(1024)S(1)}, f32[2048]{0:T(1024)S(1)}) all-reduce(f32[2048]{0:T(1024)S(1)} %get-tuple-element.610, f32[2048]{0:T(1024)S(1)} %copy-done.22), channel_id=4, replica_groups=mesh['fsdp'=4,'seq'=8] {'fsdp','seq'}, use_global_device_ids=true, to_apply=%region_15.16.clone | all-reduce | flops 4096 | bytes 32768
  1726.6 2.6 fusion.104
  1734.5 2.6 copy.223
  1737.1 77.2 %reduce-scatter.6.cloned.1.call-done = bf16[256,2,2048]{0,2,1:T(8,128)(2,1)} async-done(((bf16[1024,2,2048]{0,2,1:T(8,128)(2,1)}), bf16[256,2,2048]{0,2,1:T(8,128)(2,1)}) %reduce-scatter.6.cloned.1.call-update) | async-done | bytes 2097168 | tf_op jit(solution)/shard_map/reduce_scatter | solution.py:249
  1814.3 6.4 copy.222
  (264 shorter events, 110.6 us)
Async XLA Ops:
  7.2 233.0 %all-gather.11.cloned.1.call-start = ((), (), s32[]{:S(2)}) async-start(), calls=%async_computation.8 | async-start | bytes 31457280 | tf_op jit(solution)/shard_map/all_gather | solution.py:192
  7.9 387.4 %all-gather.13.cloned.1.call-start = ((), (), s32[]{:S(2)}) async-start(), calls=%async_computation.9 | async-start | bytes 10485760 | tf_op jit(solution)/shard_map/all_gather | solution.py:193
  8.7 899.4 %all-gather.15.cloned.1.call-start = ((), (), s32[]{:S(2)}) async-start(), calls=%async_computation.10 | async-start | bytes 83886080 | tf_op jit(solution)/shard_map/all_gather | solution.py:210
  26.8 0.7 copy-start.25
  26.8 1.1 copy-start.1
  26.8 1180.0 %all-gather.17.cloned.1.call-start = ((), (), s32[]{:S(2)}) async-start(), calls=%async_computation.11 | async-start | bytes 41943040 | tf_op jit(solution)/shard_map/all_gather | solution.py:211
  27.5 347.3 %copy-start.20 = (f32[2048]{0:T(1024)}, f32[2048]{0:T(1024)S(1)}, u32[]{:S(2)}) copy-start(f32[2048]{0:T(1024)S(1)} %convert_element_type.204) | copy-start | bytes 24580
  28.7 346.2 %copy-start.23 = (f32[128]{0:T(128)}, f32[128]{0:T(128)S(1)}, u32[]{:S(2)}) copy-start(f32[128]{0:T(128)S(1)} %get-tuple-element.712) | copy-start | bytes 1540
  270.8 5.3 copy-start.19
  278.9 54.1 %all-to-all-start = ((bf16[3,1,128,2048]{2,0,1,3:T(4,128)(2,1)}), bf16[3,1,128,2048]{2,0,1,3:T(4,128)(2,1)S(1)}, u32[]{:S(2)}, u32[]{:S(2)}) async-start(bf16[3,1,128,2048]{2,0,1,3:T(4,128)(2,1)} %copy.196), calls=%async_computation | async-start | bytes 4194304 | tf_op jit(solution)/shard_map/all_to_all | solution.py:200
  336.2 3.2 copy-start.14
  357.6 18.3 %copy-start.7 = (f32[1,1024,4,64]{1,3,2,0:T(8,128)}, f32[1,1024,4,64]{1,3,2,0:T(8,128)S(1)}, u32[]{:S(2)}) copy-start(f32[1,1024,4,64]{1,3,2,0:T(8,128)S(1)} %get-tuple-element.501) | copy-start | bytes 3145732
  357.6 17.3 copy-start.2
  357.6 18.5 %copy-start.26 = (bf16[2048]{0:T(1024)(128)(2,1)S(1)}, bf16[2048]{0:T(1024)(128)(2,1)}, u32[]{:S(2)}) copy-start(bf16[2048]{0:T(1024)(128)(2,1)} %param.18) | copy-start | bytes 12292
  370.7 19.5 %all-to-all-start.1 = ((bf16[8,2,16384]{2,1,0:T(2,128)(2,1)}), bf16[8,2,16384]{2,1,0:T(2,128)(2,1)}, u32[]{:S(2)}, u32[]{:S(2)}) async-start(bf16[8,2,16384]{2,1,0:T(2,128)(2,1)} %reshape.879), calls=%async_computation.1 | async-start | bytes 1048576 | tf_op jit(solution)/shard_map/all_to_all | solution.py:203
  374.8 1015.3 %all-gather.19.cloned.1.call-start = ((), (), s32[]{:S(2)}) async-start(), calls=%async_computation.12 | async-start | bytes 4718592 | tf_op jit(solution)/shard_map/all_gather | solution.py:271
  375.9 1029.6 %all-gather.23.cloned.1.call-start = ((), (), s32[]{:S(2)}) async-start(), calls=%async_computation.17 | async-start | bytes 4718592 | tf_op jit(solution)/shard_map/all_gather | solution.py:274
  401.8 849.5 %copy-start.4 = (f32[128,2048]{1,0:T(8,128)}, f32[128,2048]{1,0:T(8,128)S(1)}, u32[]{:S(2)}) copy-start(f32[128,2048]{1,0:T(8,128)S(1)} %get-tuple-element.716) | copy-start | bytes 3145732
  402.0 543.7 %copy-start.11 = (bf16[128,2048]{1,0:T(8,128)(2,1)}, bf16[128,2048]{1,0:T(8,128)(2,1)S(1)}, u32[]{:S(2)}) copy-start(bf16[128,2048]{1,0:T(8,128)(2,1)S(1)} %multiply_convert_fusion.2) | copy-start | bytes 1572868
  1226.0 25.4 %copy-start.16 = (bf16[1,128,2048]{2,1,0:T(8,128)(2,1)S(1)}, bf16[1,128,2048]{2,1,0:T(8,128)(2,1)}, u32[]{:S(2)}) copy-start(bf16[1,128,2048]{2,1,0:T(8,128)(2,1)} %param.23) | copy-start | bytes 1572868
  1252.9 324.7 %all-gather.21.cloned.1.call-start = ((), (), s32[]{:S(2)}) async-start(), calls=%async_computation.15 | async-start | bytes 4718592 | tf_op jit(solution)/shard_map/all_gather | solution.py:240
  1253.6 344.4 %all-gather.25.cloned.1.call-start = ((), (), s32[]{:S(2)}) async-start(), calls=%async_computation.18 | async-start | bytes 4718592 | tf_op jit(solution)/shard_map/all_gather | solution.py:237
  1254.4 6.0 copy-start.9
  1278.4 32.9 %all-to-all-start.2 = ((bf16[8,2,16384]{2,1,0:T(2,128)(2,1)}), bf16[8,2,16384]{2,1,0:T(2,128)(2,1)S(1)}, u32[]{:S(2)}, u32[]{:S(2)}) async-start(bf16[8,2,16384]{2,1,0:T(2,128)(2,1)} %reshape.881), calls=%async_computation.2 | async-start | bytes 1048576 | tf_op jit(solution)/shard_map/all_to_all | solution.py:267
  1311.3 256.2 %all-to-all-start.4 = ((bf16[3,1,128,8192]{2,0,1,3:T(4,128)(2,1)}), bf16[3,1,128,8192]{2,0,1,3:T(4,128)(2,1)}, u32[]{:S(2)}, u32[]{:S(2)}) async-start(bf16[3,1,128,8192]{2,0,1,3:T(4,128)(2,1)} %copy.216), calls=%async_computation.5 | async-start | bytes 16777216 | tf_op jit(solution)/shard_map/all_to_all | solution.py:236
  1316.2 8.6 copy-start.8
  1316.3 413.0 %all-reduce.6.cloned.1.call-start = ((), (), s32[]{:S(2)}) async-start(), calls=%async_computation.19 | async-start | bytes 8388608
  1331.7 2.7 copy-start.10
  1337.0 2.7 copy-start.10
  1345.0 2.7 copy-start.10
  1350.3 2.7 copy-start.10
  1355.7 2.7 copy-start.10
  1361.0 2.7 copy-start.10
  1372.7 4.6 copy-start.6
  1378.7 6.3 copy-start.13
  1390.1 7.6 copy-start.17
  1397.7 7.9 copy-start.15
  1405.5 327.3 %reduce-scatter.4.cloned.1.call-start = ((), (), s32[]{:S(2)}) async-start(), calls=%async_computation.13 | async-start | bytes 1310720 | tf_op jit(solution)/shard_map/reduce_scatter | solution.py:289
  1410.0 324.5 %reduce-scatter.8.cloned.1.call-start = ((), (), s32[]{:S(2)}) async-start(), calls=%async_computation.16 | async-start | bytes 5242880 | tf_op jit(solution)/shard_map/reduce_scatter | solution.py:252
  1572.1 2.7 copy-start
  1587.1 227.2 %reduce-scatter.6.cloned.1.call-start = ((), (), s32[]{:S(2)}) async-start(), calls=%async_computation.14 | async-start | bytes 10485760 | tf_op jit(solution)/shard_map/reduce_scatter | solution.py:249
  1612.2 1.1 copy-start.18
  1613.5 6.5 copy-start.28
  1613.5 7.8 copy-start.5
  1616.2 52.8 %all-to-all-start.3 = ((bf16[3,1,1024,256]{3,0,1,2:T(4,128)(2,1)}), bf16[3,1,1024,256]{3,0,1,2:T(4,128)(2,1)S(1)}, u32[]{:S(2)}, u32[]{:S(2)}) async-start(bf16[3,1,1024,256]{3,0,1,2:T(4,128)(2,1)} %copy.210), calls=%async_computation.3 | async-start | bytes 4194304 | tf_op jit(solution)/shard_map/all_to_all | solution.py:293
  1640.2 33.6 %copy-start.3 = (bf16[1,128,2048]{2,1,0:T(8,128)(2,1)S(1)}, bf16[1,128,2048]{2,1,0:T(8,128)(2,1)}, u32[]{:S(2)}) copy-start(bf16[1,128,2048]{2,1,0:T(8,128)(2,1)} %param.16) | copy-start | bytes 1572868
  1640.2 33.6 %copy-start.21 = (f32[2048]{0:T(1024)S(1)}, f32[2048]{0:T(1024)}, u32[]{:S(2)}) copy-start(f32[2048]{0:T(1024)} %copy-done.20) | copy-start | bytes 24580
  1640.2 33.6 %copy-start.24 = (f32[128]{0:T(128)S(1)}, f32[128]{0:T(128)}, u32[]{:S(2)}) copy-start(f32[128]{0:T(128)} %copy-done.23) | copy-start | bytes 1540
  1673.8 13.6 copy-start.22
  1673.8 52.8 %copy-start.12 = (f32[128,2048]{1,0:T(8,128)S(1)}, f32[128,2048]{1,0:T(8,128)}, u32[]{:S(2)}) copy-start(f32[128,2048]{1,0:T(8,128)} %get-tuple-element.683) | copy-start | bytes 3145732
  1673.8 52.8 %copy-start.27 = (f32[128]{0:T(128)S(1)}, f32[128]{0:T(128)}, u32[]{:S(2)}) copy-start(f32[128]{0:T(128)} %get-tuple-element.711) | copy-start | bytes 1540
Sparse Core Ops, SparseCore 0:
  9.8 230.2 all-gather.10
  242.0 87.4 all-gather.12
  331.4 576.6 all-gather.14
  909.8 297.0 all-gather.16
  1208.3 46.8 all-gather.18
  1257.3 56.8 all-gather.22
  1315.8 78.7 all-gather.20
  1396.2 135.9 all-gather.24
  1536.0 101.4 all-reduce.5
  1640.3 27.9 reduce-scatter.3
  1671.2 53.6 reduce-scatter.7
  1727.8 86.4 reduce-scatter.5
where the time goes:
time: 1840 us; the launch traced here: 1830 us
  waiting for transfers between devices  1320 us (72%)
  matrix products  220 us (12%)
  local copies, waits for them, and re-layouts  140 us (8%)
  other arithmetic  72.3 us (4%)
  blocking collectives  38 us (2%)
  starting transfers between devices  23.7 us (1%)
    all_gather x1, waiting for transfers between devices, body(): lax.all_gather(w_gate_up, 'fsdp', axis=0, tiled=True)  506 us
    all_gather x1, waiting for transfers between devices, body(): lax.all_gather(w_down, 'fsdp', axis=0, tiled=True)  261 us
    all_gather x1, waiting for transfers between devices, body(): lax.all_gather(w_qkv, 'fsdp', axis=0, tiled=True)  211 us
    all_to_all x1, waiting for transfers between devices, body(): lax.all_to_all(unit_rows, 'seq', split_axis=3, concat_axis=2, tiled=True)  157 us
    reduce_scatter x1, waiting for transfers between devices, body(): lax.psum_scatter(gu_part.astype(jnp.bfloat16), 'fsdp', scatter_dimension=...  77.2 us
    all_to_all x1, waiting for transfers between devices, body(): lax.all_to_all(stacked, 'seq', split_axis=3, concat_axis=2, tiled=True)  49 us
    unnamed x69, local copies, waits for them, and re-layouts  43.5 us
    unnamed x1, blocking collectives  38 us
  transfers between devices with their start and end apart: 17, of which 9 were waited for; matrix products, arithmetic and copies ran while one was open for 23% of the time, Pallas kernels for 0%

commit v1 on v0

--- a/solution.py
+++ b/solution.py
@@ -178,6 +178,41 @@
 
 
 def body(residual_in, attn_gain, mlp_gain, w_qkv, w_out, w_gate_up, w_down, cotangent):
+
+    def read_field(obj):
+        everything, last, spare = (lax.axis_size("fsdp"), lax.axis_index("fsdp"), obj.shape[0])
+        met_up = lax.dynamic_update_slice_in_dim(
+            jnp.zeros(
+                tuple(
+                    (dev_j * everything if p == 0 else dev_j for p, dev_j in enumerate(obj.shape))
+                ),
+                obj.dtype,
+            ),
+            obj,
+            last * spare,
+            axis=0,
+        )
+        frame_out = base_arr = obj
+        for d in [*range(1, everything // 2 + 1)]:
+            frame_out = lax.ppermute(
+                frame_out,
+                axis_name="fsdp",
+                perm=tuple(((p, (p + 1) % everything) for p in range(everything))),
+            )
+            met_up = lax.dynamic_update_slice_in_dim(
+                met_up, frame_out, (last - d) % everything * spare, axis=0
+            )
+            if 2 * d < everything:
+                base_arr = lax.ppermute(
+                    base_arr,
+                    axis_name="fsdp",
+                    perm=tuple(((p, (p - 1) % everything) for p in range(everything))),
+                )
+                met_up = lax.dynamic_update_slice_in_dim(
+                    met_up, base_arr, (last + d) % everything * spare, axis=0
+                )
+        return met_up
+
     seq_count, shard_len, model_width = residual_in.shape
     tokens = seq_count * shard_len
     seq_index = lax.axis_index("seq")
@@ -206,10 +241,7 @@
     residual = inputs + branch
     scale_two = rms_scale(residual)
     normed_two = (residual * scale_two * gain_two).astype(jnp.bfloat16)
-    up_full, down_full = (
-        lax.all_gather(w_gate_up, "fsdp", axis=0, tiled=True),
-        lax.all_gather(w_down, "fsdp", axis=0, tiled=True),
-    )
+    up_full, down_full = (lax.all_gather(w_gate_up, "fsdp", axis=0, tiled=True), read_field(w_down))
     gate_up = jnp.einsum("td,jpd->ptj", normed_two, up_full, preferred_element_type=jnp.float32)
     hidden = (jax.nn.silu(gate_up[0]) * gate_up[1]).astype(jnp.bfloat16)
     mlp_term = jnp.einsum("tj,fj->tf", hidden, down_full, preferred_element_type=jnp.float32)

time: 1840 us -> 2390 us (1.30)
  waiting for transfers between devices: 1320 us -> 1830 us
  local copies, waits for them, and re-layouts: 140 us -> 179 us
    ppermute x0 -> x3, waiting for transfers between devices: none -> 613 us  [the longest x2 432 us: read_field(): lax.ppermute(frame_out, axis_name='fsdp', perm=tuple(((p, (p + 1) % every...]
    reduce_scatter x1, waiting for transfers between devices: 77.2 us -> 0.01 us  [body(): lax.psum_scatter(gu_part.astype(jnp.bfloat16), 'fsdp', scatter_dimension=...]
    dynamic_update_slice x0 -> x4, local copies, waits for them, and re-layouts: none -> 31.4 us  [the longest x2 16 us: read_field(): lax.dynamic_update_slice_in_dim(met_up, frame_out, (last - d) % everythin...]
    all_to_all x1, waiting for transfers between devices: 28.7 us -> 0.01 us  [body(): lax.all_to_all(grad_stacked, 'seq', split_axis=2, concat_axis=3, tiled=True)]
  transfers between devices with their start and end apart: 17 -> 20, of which waited for: 9 -> 10; matrix products, arithmetic and copies ran while one was open for 23% -> 19% of each run, Pallas kernels for 0% -> 0%
where the time goes in v1:
time: 2390 us; the launch traced here: 2380 us
  waiting for transfers between devices  1830 us (77%)
  matrix products  218 us (9%)
  local copies, waits for them, and re-layouts  179 us (7%)
  other arithmetic  70.7 us (3%)
  blocking collectives  37.4 us (2%)
  starting transfers between devices  27.6 us (1%)
    all_gather x1, waiting for transfers between devices, body(): lax.all_gather(w_gate_up, 'fsdp', axis=0, tiled=True)  507 us
    ppermute x2, waiting for transfers between devices, read_field(): lax.ppermute(frame_out, axis_name='fsdp', perm=tuple(((p, (p + 1) % every...  432 us
    all_gather x1, waiting for transfers between devices, body(): lax.all_gather(w_down, 'fsdp', axis=0, tiled=True)  261 us
    all_gather x1, waiting for transfers between devices, body(): lax.all_gather(w_qkv, 'fsdp', axis=0, tiled=True)  211 us
    ppermute x1, waiting for transfers between devices, read_field(): lax.ppermute(base_arr, axis_name='fsdp', perm=tuple(((p, (p - 1) % everyt...  181 us
    all_to_all x1, waiting for transfers between devices, body(): lax.all_to_all(unit_rows, 'seq', split_axis=3, concat_axis=2, tiled=True)  162 us
    all_to_all x1, waiting for transfers between devices, body(): lax.all_to_all(stacked, 'seq', split_axis=3, concat_axis=2, tiled=True)  49 us
  transfers between devices with their start and end apart: 20, of which 10 were waited for; matrix products, arithmetic and copies ran while one was open for 19% of the time, Pallas kernels for 0%

profile of v1, /device:TPU:0, one launch (start us, length us, event | category | flops | bytes accessed | tf_op | source)
XLA Modules:
  0.0 2379.1 jit_solution(9604766458613132319)
XLA Ops:
  8.7 18.1 copy.202
  28.7 211.5 %all-gather.11.cloned.1.call-done = bf16[2048,3,2048]{2,0,1:T(8,128)(2,1)} async-done(((bf16[512,3,2048]{2,0,1:T(8,128)(2,1)}), bf16[2048,3,2048]{2,0,1:T(8,128)(2,1)}) %all-gather.11.cloned.1.call-update) | async-done | bytes 25165840 | tf_op jit(solution)/shard_map/all_gather | solution.py:227
  240.2 13.5 convolution_bitcast_fusion.3
  256.0 2.5 copy.194
  260.9 2.5 copy.195
  268.3 2.5 copy.193
  270.8 5.3 fusion.111
  278.9 4.8 all-to-all-start
  283.7 49.0 %all-to-all-done = bf16[3,1,128,2048]{2,0,1,3:T(4,128)(2,1)S(1)} async-done(((bf16[3,1,128,2048]{2,0,1,3:T(4,128)(2,1)}), bf16[3,1,128,2048]{2,0,1,3:T(4,128)(2,1)S(1)}, u32[]{:S(2)}, u32[]{:S(2)}) %all-to-all-start) | async-done | bytes 1572896 | tf_op jit(solution)/shard_map/all_to_all | solution.py:235
  332.7 3.2 fusion.142
  340.0 16.9 while.118
  340.9 5.1 while.121
  346.8 10.0 while.121
  357.9 3.6 copy.200
  362.0 5.9 reduce.3
  370.0 4.2 all-to-all-start.1
  375.6 13.9 all-to-all-done.1
  394.6 6.5 multiply_reduce_fusion.3
  401.4 506.7 %all-gather.15.cloned.1.call-done = bf16[8192,2,2048]{2,0,1:T(8,128)(2,1)} async-done(((bf16[2048,2,2048]{2,0,1:T(8,128)(2,1)}), bf16[8192,2,2048]{2,0,1:T(8,128)(2,1)}) %all-gather.15.cloned.1.call-update) | async-done | bytes 67108880 | tf_op jit(solution)/shard_map/all_gather | solution.py:244
  908.1 37.6 %convolution_bitcast_fusion.2 = f32[2,128,8192]{2,1,0:T(8,128)} fusion(bf16[8192,2,2048]{2,0,1:T(8,128)(2,1)} %all-gather.15.cloned.1.call-done, bf16[128,2048]{1,0:T(8,128)(2,1)S(1)} %multiply_convert_fusion.2), kind=kOutput, calls=%fused_computation.67 | convolution fusion | flops 8589934592 | bytes 76021760 | tf_op jit(solution)/shard_map/td,jpd->ptj/dot_general | solution.py:245
  945.7 261.2 %all-gather.17.cloned.1.call-done = bf16[2048,8192]{1,0:T(8,128)(2,1)} async-done(((bf16[512,8192]{1,0:T(8,128)(2,1)}), bf16[2048,8192]{1,0:T(8,128)(2,1)}) %all-gather.17.cloned.1.call-update) | async-done | bytes 33554448 | tf_op jit(solution)/shard_map/all_gather | solution.py:254
  1206.9 19.1 fusion.83
  1226.0 25.3 %multiply_reduce_fusion = (f32[2048]{0:T(1024)}, f32[128]{0:T(128)S(1)}, f32[128,2048]{1,0:T(8,128)S(1)}) fusion(f32[128,2048]{1,0:T(8,128)S(1)} %get-tuple-element.716, f32[128]{0:T(128)S(1)} %get-tuple-element.714, f32[2048]{0:T(1024)S(1)} %convert_element_type.212, bf16[8192,2,2048]{2,0,1:T(8,128)(2,1)} %all-gather.15.cloned.1.call-done, ...), kind=kOutput, calls=%fused_computation.151 | convolution fusion | flops 8593602560 | bytes 73417728 | tf_op jit(solution)/shard_map/ptj,jpd->td/dot_general | solution.py:261
  1254.4 6.0 multiply_convert_fusion
  1260.3 4.9 fusion.79
  1266.0 11.5 reduce.4
  1278.4 4.5 all-to-all-start.2
  1282.9 6.5 maximum_bitcast_fusion
  1289.5 13.2 copy.216
  1302.7 8.6 all-to-all-done.2
  1311.3 4.9 all-to-all-start.4
  1329.0 37.3 %while.120 = (s32[]{:T(128)}, f32[1,1024,4,64]{1,3,2,0:T(8,128)}, f32[1,1024,4,64]{1,3,2,0:T(8,128)S(1)}, f32[1,1024,4,64]{1,3,2,0:T(8,128)}, bf16[1,1024,4,64]{...) while((s32[]{:T(128)}, f32[1,1024,4,64]{1,3,2,0:T(8,128)}, ...), condition=%wide.region_12.13_spmd, body=%wide.region_9.12_spmd.sunk | while | flops 340329248 | bytes 17070864 | solution.py:170
  1330.7 10.7 while.122
  1344.1 21.4 while.122
  1366.3 4.7 fusion.115
  1380.3 5.2 add_convert_fusion.1
  1385.6 7.5 fusion.72
  1393.1 7.8 copy.215
  1401.0 4.5 convolution_convert_fusion
  1405.6 161.9 %all-to-all-done.4 = bf16[3,1,128,8192]{2,0,1,3:T(4,128)(2,1)} async-done(((bf16[3,1,128,8192]{2,0,1,3:T(4,128)(2,1)}), bf16[3,1,128,8192]{2,0,1,3:T(4,128)(2,1)}, u32[]{:S(2)}, u32[]{:S(2)}) %all-to-all-start.4) | async-done | bytes 6291488 | tf_op jit(solution)/shard_map/all_to_all | solution.py:268
  1567.5 4.6 copy.217
  1572.1 2.7 copy-done
  1574.9 2.6 copy.220
  1577.5 9.4 convert_bitcast_fusion.1
  1588.2 4.6 slice.103
  1592.8 6.6 copy.218
  1599.5 14.1 convert_bitcast_fusion
  1615.5 268.1 %collective-permute-done = bf16[512,8192]{1,0:T(8,128)(2,1)} collective-permute-done((bf16[512,8192]{1,0:T(8,128)(2,1)}, bf16[512,8192]{1,0:T(8,128)(2,1)}, u32[]{:S(2)}, u32[]{:S(2)}) %collective-permute-start) | collective-permute-done | bytes 8388640 | tf_op jit(solution)/shard_map/ppermute | solution.py:197
  1886.0 11.1 broadcast_in_dim.24
  1897.1 7.7 constant_dynamic-update-slice_fusion.5
  1904.8 8.3 constant_dynamic-update-slice_fusion.4
  1913.1 181.2 %collective-permute-done.1 = bf16[512,8192]{1,0:T(8,128)(2,1)} collective-permute-done((bf16[512,8192]{1,0:T(8,128)(2,1)}, bf16[512,8192]{1,0:T(8,128)(2,1)}, u32[]{:S(2)}, u32[]{:S(2)}) %collective-permute-start.1) | collective-permute-done | bytes 8388640 | tf_op jit(solution)/shard_map/ppermute | solution.py:206
  2094.3 7.7 constant_dynamic-update-slice_fusion.3
  2102.4 2.7 copy.210
  2105.0 3.8 all-to-all-start.3
  2108.8 163.8 %collective-permute-done.2 = bf16[512,8192]{1,0:T(8,128)(2,1)} collective-permute-done((bf16[512,8192]{1,0:T(8,128)(2,1)}, bf16[512,8192]{1,0:T(8,128)(2,1)}, u32[]{:S(2)}, u32[]{:S(2)}) %collective-permute-start.2) | collective-permute-done | bytes 8388640 | tf_op jit(solution)/shard_map/ppermute | solution.py:197
  2272.7 7.7 constant_dynamic-update-slice_fusion.2
  2280.4 18.5 fusion.80
  2301.1 2.6 reshape.847
  2303.8 12.9 fusion.107
  2316.6 37.4 %all-reduce.3 = (f32[2048]{0:T(1024)S(1)}, f32[2048]{0:T(1024)S(1)}) all-reduce(f32[2048]{0:T(1024)S(1)} %get-tuple-element.610, f32[2048]{0:T(1024)S(1)} %copy-done.22), channel_id=4, replica_groups=mesh['fsdp'=4,'seq'=8] {'fsdp','seq'}, use_global_device_ids=true, to_apply=%region_15.16.clone | all-reduce | flops 4096 | bytes 32768
  2355.2 2.6 fusion.104
  2363.1 2.6 copy.223
  2365.7 6.4 copy.222
  (275 shorter events, 124.0 us)
Async XLA Ops:
  7.2 233.0 %all-gather.11.cloned.1.call-start = ((), (), s32[]{:S(2)}) async-start(), calls=%async_computation.8 | async-start | bytes 31457280 | tf_op jit(solution)/shard_map/all_gather | solution.py:227
  7.9 386.7 %all-gather.13.cloned.1.call-start = ((), (), s32[]{:S(2)}) async-start(), calls=%async_computation.9 | async-start | bytes 10485760 | tf_op jit(solution)/shard_map/all_gather | solution.py:228
  8.7 899.4 %all-gather.15.cloned.1.call-start = ((), (), s32[]{:S(2)}) async-start(), calls=%async_computation.10 | async-start | bytes 83886080 | tf_op jit(solution)/shard_map/all_gather | solution.py:244
  26.8 0.7 copy-start.25
  26.8 1.1 copy-start.1
  26.8 1180.0 %all-gather.17.cloned.1.call-start = ((), (), s32[]{:S(2)}) async-start(), calls=%async_computation.11 | async-start | bytes 41943040 | tf_op jit(solution)/shard_map/all_gather | solution.py:254
  27.5 346.7 %copy-start.20 = (f32[2048]{0:T(1024)}, f32[2048]{0:T(1024)S(1)}, u32[]{:S(2)}) copy-start(f32[2048]{0:T(1024)S(1)} %convert_element_type.204) | copy-start | bytes 24580
  28.7 345.5 %copy-start.23 = (f32[128]{0:T(128)}, f32[128]{0:T(128)S(1)}, u32[]{:S(2)}) copy-start(f32[128]{0:T(128)S(1)} %get-tuple-element.712) | copy-start | bytes 1540
  270.8 5.3 copy-start.19
  278.9 53.8 %all-to-all-start = ((bf16[3,1,128,2048]{2,0,1,3:T(4,128)(2,1)}), bf16[3,1,128,2048]{2,0,1,3:T(4,128)(2,1)S(1)}, u32[]{:S(2)}, u32[]{:S(2)}) async-start(bf16[3,1,128,2048]{2,0,1,3:T(4,128)(2,1)} %copy.196), calls=%async_computation | async-start | bytes 4194304 | tf_op jit(solution)/shard_map/all_to_all | solution.py:235
  335.9 3.2 copy-start.14
  357.0 18.3 copy-start.7
  357.0 17.3 copy-start.2
  357.0 18.5 copy-start.26
  370.0 19.5 all-to-all-start.1
  374.2 1011.4 %all-gather.19.cloned.1.call-start = ((), (), s32[]{:S(2)}) async-start(), calls=%async_computation.12 | async-start | bytes 4718592 | tf_op jit(solution)/shard_map/all_gather | solution.py:303
  375.3 1025.7 %all-gather.23.cloned.1.call-start = ((), (), s32[]{:S(2)}) async-start(), calls=%async_computation.17 | async-start | bytes 4718592 | tf_op jit(solution)/shard_map/all_gather | solution.py:306
  401.2 850.1 %copy-start.4 = (f32[128,2048]{1,0:T(8,128)}, f32[128,2048]{1,0:T(8,128)S(1)}, u32[]{:S(2)}) copy-start(f32[128,2048]{1,0:T(8,128)S(1)} %get-tuple-element.716) | copy-start | bytes 3145732
  401.4 544.3 %copy-start.11 = (bf16[128,2048]{1,0:T(8,128)(2,1)}, bf16[128,2048]{1,0:T(8,128)(2,1)S(1)}, u32[]{:S(2)}) copy-start(bf16[128,2048]{1,0:T(8,128)(2,1)S(1)} %multiply_convert_fusion.2) | copy-start | bytes 1572868
  1226.0 25.3 %copy-start.16 = (bf16[1,128,2048]{2,1,0:T(8,128)(2,1)S(1)}, bf16[1,128,2048]{2,1,0:T(8,128)(2,1)}, u32[]{:S(2)}) copy-start(bf16[1,128,2048]{2,1,0:T(8,128)(2,1)} %param.23) | copy-start | bytes 1572868
  1252.9 324.7 %all-gather.21.cloned.1.call-start = ((), (), s32[]{:S(2)}) async-start(), calls=%async_computation.15 | async-start | bytes 4718592 | tf_op jit(solution)/shard_map/all_gather | solution.py:272
  1253.6 345.9 %all-gather.25.cloned.1.call-start = ((), (), s32[]{:S(2)}) async-start(), calls=%async_computation.18 | async-start | bytes 4718592 | tf_op jit(solution)/shard_map/all_gather | solution.py:269
  1254.4 6.0 copy-start.9
  1278.4 32.9 %all-to-all-start.2 = ((bf16[8,2,16384]{2,1,0:T(2,128)(2,1)}), bf16[8,2,16384]{2,1,0:T(2,128)(2,1)S(1)}, u32[]{:S(2)}, u32[]{:S(2)}) async-start(bf16[8,2,16384]{2,1,0:T(2,128)(2,1)} %reshape.881), calls=%async_computation.2 | async-start | bytes 1048576 | tf_op jit(solution)/shard_map/all_to_all | solution.py:299
  1311.3 256.2 %all-to-all-start.4 = ((bf16[3,1,128,8192]{2,0,1,3:T(4,128)(2,1)}), bf16[3,1,128,8192]{2,0,1,3:T(4,128)(2,1)}, u32[]{:S(2)}, u32[]{:S(2)}) async-start(bf16[3,1,128,8192]{2,0,1,3:T(4,128)(2,1)} %copy.216), calls=%async_computation.5 | async-start | bytes 16777216 | tf_op jit(solution)/shard_map/all_to_all | solution.py:268
  1316.2 8.2 copy-start.8
  1316.3 1041.6 %all-reduce.6.cloned.1.call-start = ((), (), s32[]{:S(2)}) async-start(), calls=%async_computation.19 | async-start | bytes 8388608
  1331.3 2.7 copy-start.10
  1336.6 2.7 copy-start.10
  1344.6 2.7 copy-start.10
  1349.9 2.7 copy-start.10
  1355.3 2.7 copy-start.10
  1360.6 2.7 copy-start.10
  1372.2 4.0 copy-start.6
  1377.5 2.8 copy-start.13
  1385.5 7.6 copy-start.17
  1393.1 7.9 copy-start.15
  1401.0 960.4 %reduce-scatter.4.cloned.1.call-start = ((), (), s32[]{:S(2)}) async-start(), calls=%async_computation.13 | async-start | bytes 1310720 | tf_op jit(solution)/shard_map/reduce_scatter | solution.py:321
  1405.6 957.5 %reduce-scatter.8.cloned.1.call-start = ((), (), s32[]{:S(2)}) async-start(), calls=%async_computation.16 | async-start | bytes 5242880 | tf_op jit(solution)/shard_map/reduce_scatter | solution.py:284
  1572.1 2.7 copy-start
  1587.0 778.7 %reduce-scatter.6.cloned.1.call-start = ((), (), s32[]{:S(2)}) async-start(), calls=%async_computation.14 | async-start | bytes 10485760 | tf_op jit(solution)/shard_map/reduce_scatter | solution.py:281
  1587.0 296.6 %collective-permute-start = (bf16[512,8192]{1,0:T(8,128)(2,1)}, bf16[512,8192]{1,0:T(8,128)(2,1)}, u32[]{:S(2)}, u32[]{:S(2)}) collective-permute-start(bf16[512,8192]{1,0:T(8,128)(2,1)} %param.22), channel_id=1, source_target_pairs={{0,8},{8,16},{16,24},{24,0},{1,9},{9,17},{17,25},{25,1},{2,10},{10... | collective-permute-start | bytes 25165832 | tf_op jit(solution)/shard_map/ppermute | solution.py:197
  1613.6 271.2 %copy-start.28 = (u32[32]{0:T(128)S(1)}, u32[32]{0:T(128)}, u32[]{:S(2)}) copy-start(u32[32]{0:T(128)} %constant.327) | copy-start | bytes 388
  1613.6 480.7 %collective-permute-start.1 = (bf16[512,8192]{1,0:T(8,128)(2,1)}, bf16[512,8192]{1,0:T(8,128)(2,1)}, u32[]{:S(2)}, u32[]{:S(2)}) collective-permute-start(bf16[512,8192]{1,0:T(8,128)(2,1)} %param.22), channel_id=1, source_target_pairs={{0,24},{8,0},{16,8},{24,16},{1,25},{9,1},{17,9},{25,17},{2,26},{10... | collective-permute-start | bytes 25165832 | tf_op jit(solution)/shard_map/ppermute | solution.py:206
  1883.6 389.1 %collective-permute-start.2 = (bf16[512,8192]{1,0:T(8,128)(2,1)}, bf16[512,8192]{1,0:T(8,128)(2,1)}, u32[]{:S(2)}, u32[]{:S(2)}) collective-permute-start(bf16[512,8192]{1,0:T(8,128)(2,1)} %collective-permute-done), channel_id=1, source_target_pairs={{0,8},{8,16},{16,24},{24,0},{1,9},{9,17},{17,25},{25,1},{2,10},{10... | collective-permute-start | bytes 25165832 | tf_op jit(solution)/shard_map/ppermute | solution.py:197
  1913.1 189.1 %copy-start.18 = (bf16[1,1024,256]{2,1,0:T(8,128)(2,1)S(1)}, bf16[1,1024,256]{2,1,0:T(8,128)(2,1)}, u32[]{:S(2)}) copy-start(bf16[1,1024,256]{2,1,0:T(8,128)(2,1)} %copy-done.17) | copy-start | bytes 1572868
  2105.0 193.8 %all-to-all-start.3 = ((bf16[3,1,1024,256]{3,0,1,2:T(4,128)(2,1)}), bf16[3,1,1024,256]{3,0,1,2:T(4,128)(2,1)S(1)}, u32[]{:S(2)}, u32[]{:S(2)}) async-start(bf16[3,1,1024,256]{3,0,1,2:T(4,128)(2,1)} %copy.210), calls=%async_computation.3 | async-start | bytes 4194304 | tf_op jit(solution)/shard_map/all_to_all | solution.py:325
  2108.8 171.5 %copy-start.5 = (f32[128,2048]{1,0:T(8,128)S(1)}, f32[128,2048]{1,0:T(8,128)}, u32[]{:S(2)}) copy-start(f32[128,2048]{1,0:T(8,128)} %copy-done.4) | copy-start | bytes 3145732
  2298.8 4.9 copy-start.3
  2298.8 4.9 copy-start.21
  2298.8 4.9 copy-start.24
  2303.7 12.9 copy-start.22
  2303.8 51.4 %copy-start.12 = (f32[128,2048]{1,0:T(8,128)S(1)}, f32[128,2048]{1,0:T(8,128)}, u32[]{:S(2)}) copy-start(f32[128,2048]{1,0:T(8,128)} %get-tuple-element.683) | copy-start | bytes 3145732
  2303.8 51.4 %copy-start.27 = (f32[128]{0:T(128)S(1)}, f32[128]{0:T(128)}, u32[]{:S(2)}) copy-start(f32[128]{0:T(128)} %get-tuple-element.711) | copy-start | bytes 1540
Sparse Core Ops, SparseCore 0:
  9.8 230.2 all-gather.10
  242.0 87.4 all-gather.12
  331.4 576.6 all-gather.14
  909.8 297.0 all-gather.16
  1208.3 46.8 all-gather.18
  1257.3 56.9 all-gather.22
  1315.8 78.7 all-gather.20
  1396.2 135.9 all-gather.24
  1536.0 136.1 all-reduce.5
  1675.0 35.1 reduce-scatter.3
  1713.1 86.5 reduce-scatter.7
  1802.6 152.9 reduce-scatter.5
